TPU v7x, 256 devices: a whole 4x4x8 slice. The times are simulated.
256 devices in a mesh: seq: 16 (over y, x), exp: 16 (over z, core).
Axes of the slice: x: 4, y: 4, z: 8, core: 2. Of those that a mesh axis runs over, the one named last changes fastest.
Arguments:
- x_in: bfloat16 [4096, 8192], P('seq', 'exp'), may hold values from -6 to 6
- z_gate: bfloat16 [4096, 8192], P('seq', 'exp'), may hold values from -6 to 6
- b_in: bfloat16 [4096, 128], P('seq'), may hold values from -0.52734375 to 0.52734375
- c_out: bfloat16 [4096, 128], P('seq'), may hold values from -0.1875 to 0.1875
- dt_step: float32 [4096, 128], P('seq', 'exp'), may hold values from 0.12 to 2052, as said below
- rate: float32 [128], P('exp'), may hold values from 0 to 0.06, as said below
- skip: float32 [128], P('exp'), may hold values from 0.5 to 1.5
- init_state: float32 [128, 64, 128], P('exp'), may hold values from -16.970562 to 16.970562
- residual: bfloat16 [4096, 8192], P(('seq', 'exp')), may hold values from -6 to 6
- norm_gain: float32 [8192], replicated, may hold values from 0.5 to 1.5
- expert_ids: int32 [4096, 2], P(('seq', 'exp')), may hold values from 0 to 15, all different within a row; in each aligned block of 16 rows (0 to 15, 16 to 31, ...) at most 3 rows name the same one
- gate_weights: float32 [4096, 2], P(('seq', 'exp')), may hold values from 0.2 to 1
- w_gate: bfloat16 [16, 8192, 2048], P('exp', None, 'seq'), may hold values from -0.0625 to 0.0625
- w_up: bfloat16 [16, 8192, 2048], P('exp', None, 'seq'), may hold values from -0.0625 to 0.0625
- w_down: bfloat16 [16, 2048, 8192], P('exp', 'seq'), may hold values from -0.125 to 0.125
Outputs:
- layer_out: bfloat16 [4096, 8192], P(('seq', 'exp'))
Inputs may be any that keep to these rules, and one draw needn't show every extreme that they name: `dt_step`: positive step sizes. `rate`: positive rates. `expert_ids`: each row names two different experts; among the rows of one device (aligned blocks of 16 rows) no expert is named by more than 3 rows, and in every draw some expert is named by exactly 3 rows of some block.
All inputs are finite; a program needn't handle non-finite values.
Results may differ from a plain program's by a relative error of at most 0.0095.
Values may be sent and summed in bfloat16 or wider, within the bound.
A program may use at most 128 MiB of HBM per device.

v0:
```python
import jax
import jax.numpy as jnp
from jax import lax
from jax.sharding import PartitionSpec as P

GROUP = 128
PRECISE = lax.Precision.HIGHEST


def entering_2(array, axis, combine, identity):
    devices, mine = (lax.axis_size(axis), lax.axis_index(axis))
    everything = jax.tree.map(
        lambda part, kind: lax.all_gather(part.astype(kind), axis),
        array,
        (jnp.bfloat16, jnp.bfloat16),
    )
    start = jax.tree.map(
        lambda part, zero: jnp.broadcast_to(jnp.asarray(zero, part.dtype), part.shape),
        array,
        identity,
    )

    def hop(k, before):
        reached = k < mine
        new = combine(
            before, jax.tree.map(lambda part, own: part[k].astype(own.dtype), everything, array)
        )
        return jax.tree.map(lambda a, b: jnp.where(reached, a, b), new, before)

    return lax.fori_loop(0, devices, hop, start)


def chain_combine(earlier, later):
    return (earlier[0] + later[0], jnp.exp(later[0])[:, None, None] * earlier[1] + later[1])


def on_device(
    x_in,
    z_gate,
    b_in,
    c_out,
    dt_step,
    rate,
    skip,
    init_state,
    residual,
    norm_gain,
    expert_ids,
    gate_weights,
    w_gate,
    w_up,
    w_down,
):
    token_count, channels = x_in.shape
    heads_here = rate.shape[0]
    head_width = channels // heads_here
    state_width = b_in.shape[1]
    blocks = token_count // GROUP
    inputs = x_in.astype(jnp.float32).reshape(blocks, GROUP, heads_here, head_width)
    keys_in = b_in.astype(jnp.float32).reshape(blocks, GROUP, state_width)
    queries = c_out.astype(jnp.float32).reshape(blocks, GROUP, state_width)
    log_steps = (-rate[None, :] * dt_step).reshape(blocks, GROUP, heads_here)
    cumulative = jnp.cumsum(log_steps, axis=1)
    scores = jnp.einsum("ctn,csn->cts", queries, keys_in, precision=PRECISE)
    causal = jnp.arange(GROUP)[:, None] >= jnp.arange(GROUP)[None, :]
    spread = cumulative[:, :, None, :] - cumulative[:, None, :, :]
    weights = jnp.exp(jnp.where(causal[None, :, :, None], spread, -jnp.inf)) * scores[..., None]
    intra_out = jnp.einsum("ctsh,cshp->cthp", weights, inputs, precision=PRECISE)
    tail_decay = jnp.exp(cumulative[:, -1:, :] - cumulative)
    block_state = jnp.einsum("csh,cshp,csn->chpn", tail_decay, inputs, keys_in, precision=PRECISE)
    block_log = cumulative[:, -1, :]

    def advance(carried, element):
        total_log, total_state = carried
        step_log, step_state = element
        updated = (
            total_log + step_log,
            jnp.exp(step_log)[:, None, None] * total_state + step_state,
        )
        return (updated, (total_log, total_state))

    zero_state = jnp.zeros((heads_here, head_width, state_width), jnp.float32)
    zero_log = jnp.zeros((heads_here,), jnp.float32)
    (device_log, device_state), (enter_log, enter_state) = lax.scan(
        advance, (zero_log, zero_state), (block_log, block_state)
    )
    prior_log, prior_state = entering_2(
        (device_log, device_state), "seq", chain_combine, (zero_log, zero_state)
    )
    incoming = prior_state + jnp.exp(prior_log)[:, None, None] * init_state
    entering = enter_state + jnp.exp(enter_log)[:, :, None, None] * incoming[None]
    inter_out = jnp.exp(cumulative)[..., None] * jnp.einsum(
        "chpn,ctn->cthp", entering, queries, precision=PRECISE
    )
    mixed_out = (intra_out + inter_out + skip[None, None, :, None] * inputs).reshape(
        token_count, channels
    )
    mixer = (mixed_out * jax.nn.silu(z_gate.astype(jnp.float32))).astype(jnp.bfloat16)
    token_mix = lax.all_to_all(mixer, "exp", split_axis=0, concat_axis=1, tiled=True)
    stream = (residual.astype(jnp.float32) + token_mix.astype(jnp.float32)).astype(jnp.bfloat16)
    widened = stream.astype(jnp.float32)
    normed = (
        widened
        * lax.rsqrt(jnp.mean(widened * widened, axis=-1, keepdims=True) + 1e-06)
        * norm_gain[None, :]
    ).astype(jnp.bfloat16)
    rows_here = residual.shape[0]
    owners = lax.axis_size("exp")
    local_experts = w_gate.shape[0]
    experts = owners * local_experts
    capacity = max(2, 2 * rows_here // experts + 1)
    width = residual.shape[1]
    chosen = expert_ids.reshape(-1)
    onehot = (chosen[:, None] == jnp.arange(experts)[None, :]).astype(jnp.int32)
    slot_index = jnp.sum((jnp.cumsum(onehot, axis=0) - onehot) * onehot, axis=1)
    target = chosen * capacity + slot_index
    placing = (target[None, :] == jnp.arange(experts * capacity)[:, None]).astype(jnp.bfloat16)
    pair_rows = jnp.repeat(normed, 2, axis=0)
    outgoing = jnp.dot(placing, pair_rows, preferred_element_type=jnp.float32).astype(jnp.bfloat16)
    outgoing = outgoing.reshape(owners, local_experts, 1, capacity, width)
    arrived = lax.all_to_all(outgoing, "exp", split_axis=0, concat_axis=2, tiled=True)
    segment = lax.all_gather(arrived, "seq", axis=1, tiled=True)
    flattened = segment.reshape(segment.shape[0], -1, segment.shape[-1])
    gate_proj = jnp.einsum("erd,edf->erf", flattened, w_gate, preferred_element_type=jnp.float32)
    up_proj = jnp.einsum("erd,edf->erf", flattened, w_up, preferred_element_type=jnp.float32)
    active = (jax.nn.silu(gate_proj) * up_proj).astype(jnp.bfloat16)
    partial_value = jnp.einsum("erf,efd->erd", active, w_down, preferred_element_type=jnp.float32)
    partials = partial_value.reshape(segment.shape[:-1] + (partial_value.shape[-1],))
    summed = lax.psum_scatter(partials.astype(jnp.bfloat16), "seq", scatter_dimension=1, tiled=True)
    returned = lax.all_to_all(summed, "exp", split_axis=2, concat_axis=0, tiled=True)
    results = returned.reshape(experts * capacity, width)
    picked = results[target].astype(jnp.float32).reshape(rows_here, 2, width)
    mixture = jnp.sum(picked * gate_weights[:, :, None], axis=1)
    return (widened + mixture).astype(jnp.bfloat16)


def solution(mesh):
    return jax.shard_map(
        on_device,
        mesh=mesh,
        in_specs=(
            P("seq", "exp"),
            P("seq", "exp"),
            P("seq", None),
            P("seq", None),
            P("seq", "exp"),
            P("exp"),
            P("exp"),
            P("exp", None, None),
            P(("seq", "exp"), None),
            P(),
            P(("seq", "exp"), None),
            P(("seq", "exp"), None),
            P("exp", None, "seq"),
            P("exp", None, "seq"),
            P("exp", "seq", None),
        ),
        out_specs=P(("seq", "exp"), None),
        check_vma=False,
    )
```

profile of v0, /device:TPU:1, one launch (start us, length us, event | category | flops | bytes accessed | tf_op | source)
XLA Modules:
  0.0 454.0 jit_solution(192723632810441709)
XLA Ops:
  6.6 0.8 neg.13
  7.4 0.8 multiply_bitcast_fusion
  8.6 1.3 reshape.209
  9.9 0.3 copy.79
  10.2 0.4 fusion.24
  10.6 4.3 while.33
  10.7 0.7 bitcast_dynamic-update-slice_fusion.2
  11.5 1.3 dynamic_update_slice.14
  12.8 0.7 bitcast_dynamic-update-slice_fusion.2
  13.6 1.3 dynamic_update_slice.14
  14.9 0.7 convert_element_type.91
  15.6 0.7 copy.76
  16.3 1.3 dynamic-slice
  18.2 0.2 dynamic-update-slice
  18.5 34.4 %all-reduce = bf16[128]{0:T(256)(128)(2,1)S(1)} all-reduce(bf16[128]{0:T(256)(128)(2,1)S(1)} %dynamic-update-slice), channel_id=2, replica_groups=mesh['seq'=16,'exp'=16] {'seq'}, use_global_device_ids=true, to_apply=%add | all-reduce | flops 128 | bytes 512
  52.9 0.7 exp.49
  53.7 1.1 copy.84
  55.2 13.5 %all-gather.6.cloned.1.call-done = bf16[128,64,128]{2,1,0:T(8,128)(2,1)} async-done(((bf16[8,64,128]{2,1,0:T(8,128)(2,1)}), bf16[128,64,128]{2,1,0:T(8,128)(2,1)}) %all-gather.6.cloned.1.call-update) | async-done | bytes 2097168 | tf_op jit(solution)/shard_map/all_gather | solution.py:13
  68.7 17.0 %while.34 = (s32[]{:T(128)}, f32[8]{0:T(128)S(1)}, f32[8,64,128]{2,1,0:T(8,128)S(1)}, s32[]{:T(128)}, bf16[16,8]{1,0:T(8,128)(2,1)S(1)}, /*index=5*/bf16[16,8,64,128]{3,2,1,0:T(8,128)(2,1)}, s32[]{:T(128)}, s32[]{:T(128)}) while((s32[]{:T(128)}, f32[8]{0:T(128)S(1)}, f32[8,64,128]{2,1,0:T(8,128)S(1)}, s32[]{:T(128)}, ...), condition=%wide.region_4.5_spmd.clone, body=%wide.region_3.4_spmd.clone.sunk | while | flops 327716 | bytes 655619 | solution.py:30
  68.7 1.0 fusion.62
  69.8 1.0 fusion.62
  70.8 1.0 fusion.62
  71.9 1.0 fusion.62
  73.0 1.0 fusion.62
  74.0 1.0 fusion.62
  75.1 1.0 fusion.62
  76.1 1.0 fusion.62
  77.2 1.0 fusion.62
  78.3 1.0 fusion.62
  79.3 1.0 fusion.62
  80.4 1.0 fusion.62
  81.4 1.0 fusion.62
  82.5 1.0 fusion.62
  83.6 1.0 fusion.62
  84.6 1.0 fusion.62
  85.7 1.0 multiply_add_fusion
  86.7 1.5 fusion.13
  88.2 1.3 fusion.12
  89.6 0.4 copy.83
  90.2 0.8 copy.85
  91.0 8.5 %all-to-all-start = ((bf16[16,16,512]{2,1,0:T(8,128)(2,1)}), bf16[16,16,512]{2,1,0:T(8,128)(2,1)S(1)}, u32[]{:S(2)}, u32[]{:S(2)}) async-start(bf16[16,16,512]{2,1,0:T(8,128)(2,1)} %bitcast.12), calls=%async_computation | async-start | bytes 524288 | tf_op jit(solution)/shard_map/all_to_all | solution.py:99
  99.9 11.3 %all-to-all-done = bf16[16,16,512]{2,1,0:T(8,128)(2,1)S(1)} async-done(((bf16[16,16,512]{2,1,0:T(8,128)(2,1)}), bf16[16,16,512]{2,1,0:T(8,128)(2,1)S(1)}, u32[]{:S(2)}, u32[]{:S(2)}) %all-to-all-start) | async-done | bytes 262176 | tf_op jit(solution)/shard_map/all_to_all | solution.py:99
  111.7 0.4 broadcast_in_dim.34
  112.4 1.2 convolution_convert_fusion.1
  113.6 1.5 reshape.174
  115.1 31.2 %all_to_all.34 = bf16[16,1,1,3,8192]{4,3,2,1,0:T(4,128)(2,1)S(1)} all-to-all(bf16[16,1,1,3,8192]{4,3,2,1,0:T(4,128)(2,1)S(1)} %bitcast.114), channel_id=1, replica_groups=mesh['seq'=16,'exp'=16] {'exp'}, dimensions={0} | all-to-all | bytes 1572864 | tf_op jit(solution)/shard_map/all_to_all | solution.py:121
  146.3 1.5 copy.89
  148.0 89.6 %all-gather.8.cloned.1.call-done = bf16[256,1,1,3,8192]{4,0,3,2,1:T(8,128)(2,1)} async-done(((bf16[16,1,1,3,8192]{4,0,3,2,1:T(8,128)(2,1)}), bf16[256,1,1,3,8192]{4,0,3,2,1:T(8,128)(2,1)}) %all-gather.8.cloned.1.call-update) | async-done | bytes 12582928 | tf_op jit(solution)/shard_map/all_gather | solution.py:122
  237.6 18.8 %copy.90 = bf16[256,1,1,3,8192]{4,3,0,2,1:T(4,128)(2,1)} copy(bf16[256,1,1,3,8192]{4,0,3,2,1:T(8,128)(2,1)} %all-gather.8.cloned.1.call-done) | data formatting | bytes 25165824 | tf_op jit(solution)/shard_map/all_gather | solution.py:122
  256.4 26.2 %reshape.175 = bf16[768,8192]{1,0:T(8,128)(2,1)} reshape(bf16[256,1,1,3,8192]{4,3,0,2,1:T(4,128)(2,1)} %copy.90) | data formatting | bytes 25165824 | tf_op jit(solution)/shard_map/reshape.2
  282.7 7.7 %fusion.9 = f32[768,128]{1,0:T(8,128)S(1)} fusion(bf16[768,8192]{1,0:T(8,128)(2,1)} %reshape.175, bf16[1,8192,128]{2,1,0:T(8,128)(2,1)} %param.31), kind=kOutput, calls=%fused_computation.21 | convolution fusion | flops 1610612736 | bytes 15073280 | tf_op jit(solution)/shard_map/erd,edf->erf/dot_general | solution.py:124
  290.4 1.0 copy-done.1
  291.4 0.6 copy-done.9
  292.0 3.4 fusion.17
  295.6 6.4 %fusion.5 = bf16[1,16,16,3,8192]{4,2,3,1,0:T(8,128)(2,1)} fusion(bf16[1,128,8192]{2,1,0:T(8,128)(2,1)S(1)} %copy-done, bf16[16,16,3,128]{3,2,1,0:T(4,128)(2,1)S(1)} %dot_general.46), kind=kOutput, calls=%fused_computation.16 | convolution fusion | flops 1616904192 | bytes 14876672 | tf_op jit(solution)/shard_map/erf,efd->erd/dot_general | solution.py:127
  302.0 99.5 %reduce-scatter.7.cloned.1.call-done = bf16[1,1,16,3,8192]{4,2,3,1,0:T(8,128)(2,1)} async-done(((bf16[1,16,16,3,8192]{4,2,3,1,0:T(8,128)(2,1)}), bf16[1,1,16,3,8192]{4,2,3,1,0:T(8,128)(2,1)}) %reduce-scatter.7.cloned.1.call-update) | async-done | bytes 786448
  401.5 2.8 copy.92
  404.2 7.9 %all-to-all-start.2 = ((bf16[1,1,16,3,8192]{4,3,1,0,2:T(4,128)(2,1)}), bf16[1,1,16,3,8192]{4,3,1,0,2:T(4,128)(2,1)}, u32[]{:S(2)}, u32[]{:S(2)}) async-start(bf16[1,1,16,3,8192]{4,3,1,0,2:T(4,128)(2,1)} %copy.92), calls=%async_computation.2 | async-start | bytes 2097152 | tf_op jit(solution)/shard_map/all_to_all | solution.py:130
  412.4 27.8 %all-to-all-done.2 = bf16[1,1,16,3,8192]{4,3,1,0,2:T(4,128)(2,1)} async-done(((bf16[1,1,16,3,8192]{4,3,1,0,2:T(4,128)(2,1)}), bf16[1,1,16,3,8192]{4,3,1,0,2:T(4,128)(2,1)}, u32[]{:S(2)}, u32[]{:S(2)}) %all-to-all-start.2) | async-done | bytes 786464 | tf_op jit(solution)/shard_map/all_to_all | solution.py:130
  440.2 1.7 reshape.179
  441.9 1.7 gather_fusion
  443.6 1.7 reshape.183
  445.3 1.4 multiply_reduce_fusion
  446.7 0.8 fusion.32
  (84 shorter events, 3.3 us)
Async XLA Ops:
  6.5 289.0 %copy-start = (bf16[1,128,8192]{2,1,0:T(8,128)(2,1)S(1)}, bf16[1,128,8192]{2,1,0:T(8,128)(2,1)}, u32[]{:S(2)}) copy-start(bf16[1,128,8192]{2,1,0:T(8,128)(2,1)} %param.33) | copy-start | bytes 6291460
  6.5 3.7 copy-start.4
  6.5 62.1 %all-gather.6.cloned.1.call-start = ((), (), s32[]{:S(2)}) async-start(), calls=%async_computation.4 | async-start | bytes 2228224 | tf_op jit(solution)/shard_map/all_gather | solution.py:13
  10.6 44.2 %copy-start.7 = (s32[16,2]{0,1:T(2,128)S(1)}, s32[16,2]{0,1:T(2,128)}, u32[]{:S(2)}) copy-start(s32[16,2]{0,1:T(2,128)} %param.29) | copy-start | bytes 388
  10.6 44.4 %copy-start.2 = (bf16[256,128]{1,0:T(8,128)(2,1)S(1)}, bf16[256,128]{1,0:T(8,128)(2,1)}, u32[]{:S(2)}) copy-start(bf16[256,128]{1,0:T(8,128)(2,1)} %param.22) | copy-start | bytes 196612
  68.7 19.5 %copy-start.6 = (f32[2,128,8]{1,2,0:T(8,128)S(1)}, f32[2,128,8]{1,2,0:T(8,128)}, u32[]{:S(2)}) copy-start(f32[2,128,8]{1,2,0:T(8,128)} %copy.76) | copy-start | bytes 24580
  68.7 19.5 %copy-start.10 = (f32[8]{0:T(128)S(1)}, f32[8]{0:T(128)}, u32[]{:S(2)}) copy-start(f32[8]{0:T(128)} %param.25) | copy-start | bytes 100
  90.0 21.4 %copy-start.3 = (bf16[16,8192]{1,0:T(8,128)(2,1)S(1)}, bf16[16,8192]{1,0:T(8,128)(2,1)}, u32[]{:S(2)}) copy-start(bf16[16,8192]{1,0:T(8,128)(2,1)} %param.27) | copy-start | bytes 786436
  90.2 21.4 %copy-start.5 = (f32[8192]{0:T(1024)S(1)}, f32[8192]{0:T(1024)}, u32[]{:S(2)}) copy-start(f32[8192]{0:T(1024)} %param.28) | copy-start | bytes 98308
  91.0 20.2 %all-to-all-start = ((bf16[16,16,512]{2,1,0:T(8,128)(2,1)}), bf16[16,16,512]{2,1,0:T(8,128)(2,1)S(1)}, u32[]{:S(2)}, u32[]{:S(2)}) async-start(bf16[16,16,512]{2,1,0:T(8,128)(2,1)} %bitcast.12), calls=%async_computation | async-start | bytes 524288 | tf_op jit(solution)/shard_map/all_to_all | solution.py:99
  99.6 138.0 %all-gather.8.cloned.1.call-start = ((), (), s32[]{:S(2)}) async-start(), calls=%async_computation.5 | async-start | bytes 13369344 | tf_op jit(solution)/shard_map/all_gather | solution.py:122
  147.8 253.7 %reduce-scatter.7.cloned.1.call-start = ((), (), s32[]{:S(2)}) async-start(), calls=%async_computation.6 | async-start | bytes 13369344
  282.7 8.8 %copy-start.1 = (bf16[768,8192]{1,0:T(8,128)(2,1)S(1)}, bf16[768,8192]{1,0:T(8,128)(2,1)}, u32[]{:S(2)}) copy-start(bf16[768,8192]{1,0:T(8,128)(2,1)} %reshape.175) | copy-start | bytes 37748740
  282.7 9.4 %copy-start.9 = (bf16[1,8192,128]{2,1,0:T(8,128)(2,1)S(1)}, bf16[1,8192,128]{2,1,0:T(8,128)(2,1)}, u32[]{:S(2)}) copy-start(bf16[1,8192,128]{2,1,0:T(8,128)(2,1)} %param.32) | copy-start | bytes 6291460
  302.0 110.4 %copy-start.8 = (f32[16,2]{0,1:T(2,128)S(1)}, f32[16,2]{0,1:T(2,128)}, u32[]{:S(2)}) copy-start(f32[16,2]{0,1:T(2,128)} %param.30) | copy-start | bytes 388
  404.2 35.9 %all-to-all-start.2 = ((bf16[1,1,16,3,8192]{4,3,1,0,2:T(4,128)(2,1)}), bf16[1,1,16,3,8192]{4,3,1,0,2:T(4,128)(2,1)}, u32[]{:S(2)}, u32[]{:S(2)}) async-start(bf16[1,1,16,3,8192]{4,3,1,0,2:T(4,128)(2,1)} %copy.92), calls=%async_computation.2 | async-start | bytes 2097152 | tf_op jit(solution)/shard_map/all_to_all | solution.py:130
Sparse Core Ops, SparseCore 0:
  15.7 52.9 all-gather.5
  147.9 89.6 all-gather.7
  302.1 99.3 reduce-scatter.6
where the time goes:
time: 456 us; the launch traced here: 454 us
  waiting for transfers between devices  242 us (53%)
  local copies, waits for them, and re-layouts  68.5 us (15%)
  blocking collectives  65.6 us (14%)
  other arithmetic  24.9 us (5%)
  matrix products  22.1 us (5%)
  starting transfers between devices  16.7 us (4%)
  between operations  14.1 us (3%)
    unnamed x4, waiting for transfers between devices  99.5 us
    all_gather x1, waiting for transfers between devices, on_device(): segment = lax.all_gather(arrived, 'seq', axis=1, tiled=True)  89.6 us
    unnamed x1, blocking collectives  34.4 us
    all_to_all x1, blocking collectives, on_device(): lax.all_to_all(outgoing, 'exp', split_axis=0, concat_axis=2, tiled=True)  31.2 us
    all_to_all x1, waiting for transfers between devices, on_device(): lax.all_to_all(summed, 'exp', split_axis=2, concat_axis=0, tiled=True)  27.8 us
    another operation x1, local copies, waits for them, and re-layouts  26.2 us
    all_gather x1, local copies, waits for them, and re-layouts, on_device(): segment = lax.all_gather(arrived, 'seq', axis=1, tiled=True)  18.8 us
    select_n x16, other arithmetic, hop(): return jax.tree.map(lambda a, b: jnp.where(reached, a, b), new, before)  16.2 us
  transfers between devices with their start and end apart: 5, of which 5 were waited for; matrix products, arithmetic and copies ran while one was open for 1% of the time, Pallas kernels for 0%

commit v1 on v0

--- a/solution.py
+++ b/solution.py
@@ -119,7 +119,16 @@
     outgoing = jnp.dot(placing, pair_rows, preferred_element_type=jnp.float32).astype(jnp.bfloat16)
     outgoing = outgoing.reshape(owners, local_experts, 1, capacity, width)
     arrived = lax.all_to_all(outgoing, "exp", split_axis=0, concat_axis=2, tiled=True)
-    segment = lax.all_gather(arrived, "seq", axis=1, tiled=True)
+    ways = lax.axis_size("seq")
+    up = [(d, (d + 1) % ways) for d in range(ways)]
+    down = [(d, (d - 1) % ways) for d in range(ways)]
+    earlier_2, later_2 = ([arrived], [arrived])
+    for _ in range(ways // 2):
+        earlier_2.append(lax.ppermute(earlier_2[-1], "seq", up))
+    for _ in range((ways - 1) // 2):
+        later_2.append(lax.ppermute(later_2[-1], "seq", down))
+    line = jnp.concatenate([*earlier_2[::-1], *later_2[1:]], axis=1)
+    segment = jnp.roll(line, (lax.axis_index("seq") - ways // 2) * arrived.shape[1], axis=1)
     flattened = segment.reshape(segment.shape[0], -1, segment.shape[-1])
     gate_proj = jnp.einsum("erd,edf->erf", flattened, w_gate, preferred_element_type=jnp.float32)
     up_proj = jnp.einsum("erd,edf->erf", flattened, w_up, preferred_element_type=jnp.float32)

time: 456 us -> 603 us (1.32); the launches traced: 454 us -> 592 us
  local copies, waits for them, and re-layouts: 68.5 us -> 133 us
  starting transfers between devices: 16.7 us -> 54 us
  waiting for transfers between devices: 242 us -> 268 us
  matrix products: 22.1 us -> 29.1 us
    ppermute x0 -> x15, waiting for transfers between devices: none -> 120 us  [the longest x8 120 us: on_device(): earlier_2.append(lax.ppermute(earlier_2[-1], 'seq', up))]
    all_gather x1 -> x0, waiting for transfers between devices: 89.6 us -> none  [on_device(): segment = lax.all_gather(arrived, 'seq', axis=1, tiled=True)]
    unnamed x28 -> x83, local copies, waits for them, and re-layouts: 4.48 us -> 78.4 us
    ppermute x0 -> x15, starting transfers between devices: none -> 37.4 us  [the longest x7 36.6 us: on_device(): later_2.append(lax.ppermute(later_2[-1], 'seq', down))]
    all_gather x1 -> x0, local copies, waits for them, and re-layouts: 18.8 us -> none  [on_device(): segment = lax.all_gather(arrived, 'seq', axis=1, tiled=True)]
    dynamic_slice x0 -> x1, local copies, waits for them, and re-layouts: none -> 12.1 us  [on_device(): jnp.roll(line, (lax.axis_index('seq') - ways // 2) * arrived.shape[1], ax...]
    unnamed x4 -> x3, waiting for transfers between devices: 99.5 us -> 96.2 us
  transfers between devices with their start and end apart: 5 -> 19, of which waited for: 5 -> 13; matrix products, arithmetic and copies ran while one was open for 1% -> 8% of each run, Pallas kernels for 0% -> 0%
where the time goes in v1:
time: 603 us; the launch traced here: 592 us
  waiting for transfers between devices  268 us (44%)
  local copies, waits for them, and re-layouts  133 us (22%)
  blocking collectives  65.8 us (11%)
  starting transfers between devices  54 us (9%)
  matrix products  29.1 us (5%)
  other arithmetic  26.6 us (4%)
  between operations  14.7 us (2%)
    ppermute x8, waiting for transfers between devices, on_device(): earlier_2.append(lax.ppermute(earlier_2[-1], 'seq', up))  120 us
    unnamed x3, waiting for transfers between devices  96.2 us
    unnamed x83, local copies, waits for them, and re-layouts  78.4 us
    ppermute x7, starting transfers between devices, on_device(): later_2.append(lax.ppermute(later_2[-1], 'seq', down))  36.6 us
    unnamed x1, blocking collectives  34.3 us
    all_to_all x1, blocking collectives, on_device(): lax.all_to_all(outgoing, 'exp', split_axis=0, concat_axis=2, tiled=True)  31.5 us
    all_to_all x1, waiting for transfers between devices, on_device(): lax.all_to_all(summed, 'exp', split_axis=2, concat_axis=0, tiled=True)  27.7 us
    another operation x1, local copies, waits for them, and re-layouts  26.3 us
  transfers between devices with their start and end apart: 19, of which 13 were waited for; matrix products, arithmetic and copies ran while one was open for 8% of the time, Pallas kernels for 0%

profile of v1, /device:TPU:1, one launch (start us, length us, event | category | flops | bytes accessed | tf_op | source)
XLA Modules:
  0.0 592.2 jit_solution(738378900589573819)
XLA Ops:
  11.4 1.8 while.33
  16.3 34.3 %all-reduce = bf16[128]{0:T(256)(128)(2,1)S(1)} all-reduce(bf16[128]{0:T(256)(128)(2,1)S(1)} %dynamic-update-slice), channel_id=2, replica_groups=mesh['seq'=16,'exp'=16] {'seq'}, use_global_device_ids=true, to_apply=%add | all-reduce | flops 128 | bytes 512
  53.9 13.1 %all-gather.4.cloned.1.call-done = bf16[128,64,128]{2,1,0:T(8,128)(2,1)} async-done(((bf16[8,64,128]{2,1,0:T(8,128)(2,1)}), bf16[128,64,128]{2,1,0:T(8,128)(2,1)}) %all-gather.4.cloned.1.call-update) | async-done | bytes 2097168 | tf_op jit(solution)/shard_map/all_gather | solution.py:13
  67.0 16.9 %while.34 = (s32[]{:T(128)}, f32[8]{0:T(128)S(1)}, f32[8,64,128]{2,1,0:T(8,128)S(1)}, s32[]{:T(128)}, bf16[16,8]{1,0:T(8,128)(2,1)S(1)}, /*index=5*/bf16[16,8,64,128]{3,2,1,0:T(8,128)(2,1)}, s32[]{:T(128)}, s32[]{:T(128)}) while((s32[]{:T(128)}, f32[8]{0:T(128)S(1)}, f32[8,64,128]{2,1,0:T(8,128)S(1)}, s32[]{:T(128)}, ...), condition=%wide.region_4.5_spmd.clone, body=%wide.region_3.4_spmd.clone.sunk | while | flops 327716 | bytes 655619 | solution.py:30
  86.5 2.0 fusion.12
  89.9 8.7 %all-to-all-start = ((bf16[16,16,512]{2,1,0:T(8,128)(2,1)}), bf16[16,16,512]{2,1,0:T(8,128)(2,1)S(1)}, u32[]{:S(2)}, u32[]{:S(2)}) async-start(bf16[16,16,512]{2,1,0:T(8,128)(2,1)} %bitcast.12), calls=%async_computation | async-start | bytes 524288 | tf_op jit(solution)/shard_map/all_to_all | solution.py:99
  99.0 11.3 %all-to-all-done = bf16[16,16,512]{2,1,0:T(8,128)(2,1)S(1)} async-done(((bf16[16,16,512]{2,1,0:T(8,128)(2,1)}), bf16[16,16,512]{2,1,0:T(8,128)(2,1)S(1)}, u32[]{:S(2)}, u32[]{:S(2)}) %all-to-all-start) | async-done | bytes 262176 | tf_op jit(solution)/shard_map/all_to_all | solution.py:99
  116.6 31.5 %all_to_all.34 = bf16[16,1,1,3,8192]{4,3,2,1,0:T(4,128)(2,1)S(1)} all-to-all(bf16[16,1,1,3,8192]{4,3,2,1,0:T(4,128)(2,1)} %bitcast.116), channel_id=1, replica_groups=mesh['seq'=16,'exp'=16] {'exp'}, dimensions={0} | all-to-all | bytes 1572864 | tf_op jit(solution)/shard_map/all_to_all | solution.py:121
  149.5 21.3 %collective-permute-done = bf16[1,1,16,3,8192]{4,2,3,1,0:T(8,128)(2,1)S(1)} collective-permute-done((bf16[1,1,16,3,8192]{4,2,3,1,0:T(8,128)(2,1)S(1)}, bf16[1,1,16,3,8192]{4,2,3,1,0:T(8,128)(2,1)S(1)}, u32[]{:S(2)}, u32[]{:S(2)}) %collective-permute-start) | collective-permute-done | bytes 786464 | tf_op jit(solution)/shard_map/ppermute | solution.py:127
  171.7 4.8 collective-permute-start.8
  176.5 17.5 %collective-permute-done.1 = bf16[1,1,16,3,8192]{4,2,3,1,0:T(8,128)(2,1)S(1)} collective-permute-done((bf16[1,1,16,3,8192]{4,2,3,1,0:T(8,128)(2,1)S(1)}, bf16[1,1,16,3,8192]{4,2,3,1,0:T(8,128)(2,1)S(1)}, u32[]{:S(2)}, u32[]{:S(2)}) %collective-permute-start.1) | collective-permute-done | bytes 786464 | tf_op jit(solution)/shard_map/ppermute | solution.py:127
  194.9 4.8 collective-permute-start.9
  199.7 15.7 %collective-permute-done.2 = bf16[1,1,16,3,8192]{4,2,3,1,0:T(8,128)(2,1)S(1)} collective-permute-done((bf16[1,1,16,3,8192]{4,2,3,1,0:T(8,128)(2,1)S(1)}, bf16[1,1,16,3,8192]{4,2,3,1,0:T(8,128)(2,1)S(1)}, u32[]{:S(2)}, u32[]{:S(2)}) %collective-permute-start.2) | collective-permute-done | bytes 786464 | tf_op jit(solution)/shard_map/ppermute | solution.py:127
  215.4 5.5 collective-permute-start.10
  220.9 14.9 %collective-permute-done.3 = bf16[1,1,16,3,8192]{4,2,3,1,0:T(8,128)(2,1)S(1)} collective-permute-done((bf16[1,1,16,3,8192]{4,2,3,1,0:T(8,128)(2,1)S(1)}, bf16[1,1,16,3,8192]{4,2,3,1,0:T(8,128)(2,1)S(1)}, u32[]{:S(2)}, u32[]{:S(2)}) %collective-permute-start.3) | collective-permute-done | bytes 786464 | tf_op jit(solution)/shard_map/ppermute | solution.py:127
  235.8 5.2 collective-permute-start.11
  241.1 14.2 %collective-permute-done.4 = bf16[1,1,16,3,8192]{4,2,3,1,0:T(8,128)(2,1)S(1)} collective-permute-done((bf16[1,1,16,3,8192]{4,2,3,1,0:T(8,128)(2,1)S(1)}, bf16[1,1,16,3,8192]{4,2,3,1,0:T(8,128)(2,1)S(1)}, u32[]{:S(2)}, u32[]{:S(2)}) %collective-permute-start.4) | collective-permute-done | bytes 786464 | tf_op jit(solution)/shard_map/ppermute | solution.py:127
  256.2 5.0 collective-permute-start.12
  261.2 12.7 %collective-permute-done.5 = bf16[1,1,16,3,8192]{4,2,3,1,0:T(8,128)(2,1)S(1)} collective-permute-done((bf16[1,1,16,3,8192]{4,2,3,1,0:T(8,128)(2,1)S(1)}, bf16[1,1,16,3,8192]{4,2,3,1,0:T(8,128)(2,1)S(1)}, u32[]{:S(2)}, u32[]{:S(2)}) %collective-permute-start.5) | collective-permute-done | bytes 786464 | tf_op jit(solution)/shard_map/ppermute | solution.py:127
  273.9 5.6 collective-permute-start.13
  279.6 12.1 %collective-permute-done.6 = bf16[1,1,16,3,8192]{4,2,3,1,0:T(8,128)(2,1)} collective-permute-done((bf16[1,1,16,3,8192]{4,2,3,1,0:T(8,128)(2,1)S(1)}, bf16[1,1,16,3,8192]{4,2,3,1,0:T(8,128)(2,1)}, u32[]{:S(2)}, u32[]{:S(2)}) %collective-permute-start.6) | collective-permute-done | bytes 786464 | tf_op jit(solution)/shard_map/ppermute | solution.py:127
  291.8 5.7 collective-permute-start.14
  297.5 11.3 %collective-permute-done.7 = bf16[1,1,16,3,8192]{4,2,3,1,0:T(8,128)(2,1)} collective-permute-done((bf16[1,1,16,3,8192]{4,2,3,1,0:T(8,128)(2,1)}, bf16[1,1,16,3,8192]{4,2,3,1,0:T(8,128)(2,1)}, u32[]{:S(2)}, u32[]{:S(2)}) %collective-permute-start.7) | collective-permute-done | bytes 786464 | tf_op jit(solution)/shard_map/ppermute | solution.py:127
  308.7 2.8 copy_dynamic-update-slice_fusion.28
  311.5 2.8 copy_dynamic-update-slice_fusion.26
  314.3 2.8 copy_dynamic-update-slice_fusion.24
  317.1 2.8 copy_dynamic-update-slice_fusion.22
  319.9 2.8 copy_dynamic-update-slice_fusion.20
  322.7 2.8 copy_dynamic-update-slice_fusion.18
  325.5 2.8 copy_dynamic-update-slice_fusion.16
  328.3 2.9 copy_dynamic-update-slice_fusion.14
  332.6 2.8 copy_dynamic-update-slice_fusion.12
  335.4 2.8 copy_dynamic-update-slice_fusion.10
  338.2 2.8 copy_dynamic-update-slice_fusion.8
  341.0 2.8 copy_dynamic-update-slice_fusion.6
  343.8 2.8 copy_dynamic-update-slice_fusion.4
  346.6 2.8 copy_dynamic-update-slice_fusion.2
  349.4 1.7 copy_dynamic-update-slice_fusion
  351.1 2.8 copy_dynamic-update-slice_fusion.29
  353.9 3.2 copy_dynamic-update-slice_fusion.27
  357.0 1.7 copy_dynamic-update-slice_fusion.25
  358.7 1.6 copy_dynamic-update-slice_fusion.23
  360.4 1.7 copy_dynamic-update-slice_fusion.21
  362.1 1.7 copy_dynamic-update-slice_fusion.19
  365.4 1.8 copy_dynamic-update-slice_fusion.15
  368.6 1.7 copy_dynamic-update-slice_fusion.13
  370.3 1.7 copy_dynamic-update-slice_fusion.11
  371.9 1.7 copy_dynamic-update-slice_fusion.9
  373.6 1.7 copy_dynamic-update-slice_fusion.7
  375.3 2.8 copy_dynamic-update-slice_fusion.5
  378.1 2.8 copy_dynamic-update-slice_fusion.3
  380.9 1.7 copy_dynamic-update-slice_fusion.1
  382.6 12.1 %constant_dynamic-slice_fusion.2 = bf16[1,16,16,3,8192]{4,3,2,1,0:T(4,128)(2,1)} fusion(bf16[1,32,16,3,8192]{4,3,2,1,0:T(4,128)(2,1)} %copy_dynamic-update-slice_fusion.1, s32[]{:T(128)S(6)} %select_n.67), kind=kLoop, calls=%fused_computation.113 | loop fusion | bytes 25165828 | tf_op jit(solution)/shard_map/jit(_roll_dynamic)/dynamic_slice | solution.py:131
  394.6 26.3 %reshape.175 = bf16[768,8192]{1,0:T(8,128)(2,1)} reshape(bf16[1,16,16,3,8192]{4,3,2,1,0:T(4,128)(2,1)} %constant_dynamic-slice_fusion.2) | data formatting | bytes 25165824 | tf_op jit(solution)/shard_map/reshape.3
  420.9 7.0 %fusion.9 = f32[768,128]{1,0:T(8,128)S(1)} fusion(bf16[768,8192]{1,0:T(8,128)(2,1)} %reshape.175, bf16[1,8192,128]{2,1,0:T(8,128)(2,1)} %param.31), kind=kOutput, calls=%fused_computation.21 | convolution fusion | flops 1610612736 | bytes 15073280 | tf_op jit(solution)/shard_map/erd,edf->erf/dot_general | solution.py:133
  428.0 8.6 %fusion.17 = bf16[768,128]{1,0:T(8,128)(2,1)S(1)} fusion(bf16[768,8192]{1,0:T(8,128)(2,1)} %reshape.175, bf16[1,8192,128]{2,1,0:T(8,128)(2,1)} %param.32, f32[768,128]{1,0:T(8,128)S(1)} %fusion.9), kind=kOutput, calls=%fused_computation.29 | convolution fusion | flops 1611202560 | bytes 15269888 | tf_op jit(solution)/shard_map/erd,edf->erf/dot_general | solution.py:134
  436.6 6.3 %fusion.5 = bf16[1,16,16,3,8192]{4,2,3,1,0:T(8,128)(2,1)} fusion(bf16[1,128,8192]{2,1,0:T(8,128)(2,1)S(1)} %copy-done, bf16[16,16,3,128]{3,2,1,0:T(4,128)(2,1)S(1)} %dot_general.46), kind=kOutput, calls=%fused_computation.16 | convolution fusion | flops 1616904192 | bytes 14876672 | tf_op jit(solution)/shard_map/erf,efd->erd/dot_general | solution.py:136
  443.0 96.2 %reduce-scatter.7.cloned.1.call-done = bf16[1,1,16,3,8192]{4,2,3,1,0:T(8,128)(2,1)} async-done(((bf16[1,16,16,3,8192]{4,2,3,1,0:T(8,128)(2,1)}), bf16[1,1,16,3,8192]{4,2,3,1,0:T(8,128)(2,1)}) %reduce-scatter.7.cloned.1.call-update) | async-done | bytes 786448
  539.2 2.8 copy.122
  542.0 7.9 %all-to-all-start.2 = ((bf16[1,1,16,3,8192]{4,3,1,0,2:T(4,128)(2,1)}), bf16[1,1,16,3,8192]{4,3,1,0,2:T(4,128)(2,1)}, u32[]{:S(2)}, u32[]{:S(2)}) async-start(bf16[1,1,16,3,8192]{4,3,1,0,2:T(4,128)(2,1)} %copy.122), calls=%async_computation.2 | async-start | bytes 2097152 | tf_op jit(solution)/shard_map/all_to_all | solution.py:139
  550.2 27.7 %all-to-all-done.2 = bf16[1,1,16,3,8192]{4,3,1,0,2:T(4,128)(2,1)} async-done(((bf16[1,1,16,3,8192]{4,3,1,0,2:T(4,128)(2,1)}), bf16[1,1,16,3,8192]{4,3,1,0,2:T(4,128)(2,1)}, u32[]{:S(2)}, u32[]{:S(2)}) %all-to-all-start.2) | async-done | bytes 786464 | tf_op jit(solution)/shard_map/all_to_all | solution.py:139
  577.9 1.7 reshape.179
  579.7 1.7 gather_fusion
  581.3 1.7 reshape.183
  (167 shorter events, 50.5 us)
Async XLA Ops:
  6.5 430.1 %copy-start = (bf16[1,128,8192]{2,1,0:T(8,128)(2,1)S(1)}, bf16[1,128,8192]{2,1,0:T(8,128)(2,1)}, u32[]{:S(2)}) copy-start(bf16[1,128,8192]{2,1,0:T(8,128)(2,1)} %param.33) | copy-start | bytes 6291460
  6.5 60.5 %all-gather.4.cloned.1.call-start = ((), (), s32[]{:S(2)}) async-start(), calls=%async_computation.4 | async-start | bytes 2228224 | tf_op jit(solution)/shard_map/all_gather | solution.py:13
  89.9 20.4 %all-to-all-start = ((bf16[16,16,512]{2,1,0:T(8,128)(2,1)}), bf16[16,16,512]{2,1,0:T(8,128)(2,1)S(1)}, u32[]{:S(2)}, u32[]{:S(2)}) async-start(bf16[16,16,512]{2,1,0:T(8,128)(2,1)} %bitcast.12), calls=%async_computation | async-start | bytes 524288 | tf_op jit(solution)/shard_map/all_to_all | solution.py:99
  98.7 440.6 %reduce-scatter.7.cloned.1.call-start = ((), (), s32[]{:S(2)}) async-start(), calls=%async_computation.5 | async-start | bytes 13369344
  148.7 22.1 %collective-permute-start = (bf16[1,1,16,3,8192]{4,2,3,1,0:T(8,128)(2,1)S(1)}, bf16[1,1,16,3,8192]{4,2,3,1,0:T(8,128)(2,1)S(1)}, u32[]{:S(2)}, u32[]{:S(2)}) collective-permute-start(bf16[1,1,16,3,8192]{4,2,3,1,0:T(8,128)(2,1)S(1)} %copy.89), channel_id=1, source_target_pairs={{0,16},{16,32},{32,48},{48,64},{64,80},{80,96},{96,112},{112,128},... | collective-permute-start | bytes 2359304 | tf_op jit(solution)/shard_map/ppermute | solution.py:127
  170.8 0.9 copy-start.1
  171.7 22.3 %collective-permute-start.1 = (bf16[1,1,16,3,8192]{4,2,3,1,0:T(8,128)(2,1)S(1)}, bf16[1,1,16,3,8192]{4,2,3,1,0:T(8,128)(2,1)S(1)}, u32[]{:S(2)}, u32[]{:S(2)}) collective-permute-start(bf16[1,1,16,3,8192]{4,2,3,1,0:T(8,128)(2,1)S(1)} %collective-permute-done), channel_id=1, source_target_pairs={{0,16},{16,32},{32,48},{48,64},{64,80},{80,96},{96,112},{112,128},... | collective-permute-start | bytes 2359304 | tf_op jit(solution)/shard_map/ppermute | solution.py:127
  171.7 22.3 %collective-permute-start.8 = (bf16[1,1,16,3,8192]{4,2,3,1,0:T(8,128)(2,1)S(1)}, bf16[1,1,16,3,8192]{4,2,3,1,0:T(8,128)(2,1)S(1)}, u32[]{:S(2)}, u32[]{:S(2)}) collective-permute-start(bf16[1,1,16,3,8192]{4,2,3,1,0:T(8,128)(2,1)S(1)} %copy.89), channel_id=1, source_target_pairs={{0,240},{16,0},{32,16},{48,32},{64,48},{80,64},{96,80},{112,96},{1... | collective-permute-start | bytes 2359304 | tf_op jit(solution)/shard_map/ppermute | solution.py:129
  194.0 21.4 %copy-start.5 = (bf16[1,1,16,3,8192]{4,2,3,1,0:T(8,128)(2,1)}, bf16[1,1,16,3,8192]{4,2,3,1,0:T(8,128)(2,1)S(1)}, u32[]{:S(2)}) copy-start(bf16[1,1,16,3,8192]{4,2,3,1,0:T(8,128)(2,1)S(1)} %collective-permute-done.1) | copy-start | bytes 2359300
  194.0 21.4 %collective-permute-start.2 = (bf16[1,1,16,3,8192]{4,2,3,1,0:T(8,128)(2,1)S(1)}, bf16[1,1,16,3,8192]{4,2,3,1,0:T(8,128)(2,1)S(1)}, u32[]{:S(2)}, u32[]{:S(2)}) collective-permute-start(bf16[1,1,16,3,8192]{4,2,3,1,0:T(8,128)(2,1)S(1)} %collective-permute-done.1), channel_id=1, source_target_pairs={{0,16},{16,32},{32,48},{48,64},{64,80},{80,96},{96,112},{112,128},... | collective-permute-start | bytes 2359304 | tf_op jit(solution)/shard_map/ppermute | solution.py:127
  194.0 0.9 copy-start.3
  194.9 20.4 %collective-permute-start.9 = (bf16[1,1,16,3,8192]{4,2,3,1,0:T(8,128)(2,1)S(1)}, bf16[1,1,16,3,8192]{4,2,3,1,0:T(8,128)(2,1)S(1)}, u32[]{:S(2)}, u32[]{:S(2)}) collective-permute-start(bf16[1,1,16,3,8192]{4,2,3,1,0:T(8,128)(2,1)S(1)} %collective-permute-done.8), channel_id=1, source_target_pairs={{0,240},{16,0},{32,16},{48,32},{64,48},{80,64},{96,80},{112,96},{1... | collective-permute-start | bytes 2359304 | tf_op jit(solution)/shard_map/ppermute | solution.py:129
  215.3 20.5 %copy-start.9 = (bf16[1,1,16,3,8192]{4,2,3,1,0:T(8,128)(2,1)}, bf16[1,1,16,3,8192]{4,2,3,1,0:T(8,128)(2,1)S(1)}, u32[]{:S(2)}) copy-start(bf16[1,1,16,3,8192]{4,2,3,1,0:T(8,128)(2,1)S(1)} %collective-permute-done.2) | copy-start | bytes 2359300
  215.3 20.4 %collective-permute-start.3 = (bf16[1,1,16,3,8192]{4,2,3,1,0:T(8,128)(2,1)S(1)}, bf16[1,1,16,3,8192]{4,2,3,1,0:T(8,128)(2,1)S(1)}, u32[]{:S(2)}, u32[]{:S(2)}) collective-permute-start(bf16[1,1,16,3,8192]{4,2,3,1,0:T(8,128)(2,1)S(1)} %collective-permute-done.2), channel_id=1, source_target_pairs={{0,16},{16,32},{32,48},{48,64},{64,80},{80,96},{96,112},{112,128},... | collective-permute-start | bytes 2359304 | tf_op jit(solution)/shard_map/ppermute | solution.py:127
  215.4 5.5 copy-start.7
  215.4 20.4 %collective-permute-start.10 = (bf16[1,1,16,3,8192]{4,2,3,1,0:T(8,128)(2,1)S(1)}, bf16[1,1,16,3,8192]{4,2,3,1,0:T(8,128)(2,1)S(1)}, u32[]{:S(2)}, u32[]{:S(2)}) collective-permute-start(bf16[1,1,16,3,8192]{4,2,3,1,0:T(8,128)(2,1)S(1)} %collective-permute-done.9), channel_id=1, source_target_pairs={{0,240},{16,0},{32,16},{48,32},{64,48},{80,64},{96,80},{112,96},{1... | collective-permute-start | bytes 2359304 | tf_op jit(solution)/shard_map/ppermute | solution.py:129
  235.8 38.2 %copy-start.15 = (bf16[1,1,16,3,8192]{4,2,3,1,0:T(8,128)(2,1)}, bf16[1,1,16,3,8192]{4,2,3,1,0:T(8,128)(2,1)S(1)}, u32[]{:S(2)}) copy-start(bf16[1,1,16,3,8192]{4,2,3,1,0:T(8,128)(2,1)S(1)} %collective-permute-done.3) | copy-start | bytes 2359300
  235.8 19.5 %collective-permute-start.4 = (bf16[1,1,16,3,8192]{4,2,3,1,0:T(8,128)(2,1)S(1)}, bf16[1,1,16,3,8192]{4,2,3,1,0:T(8,128)(2,1)S(1)}, u32[]{:S(2)}, u32[]{:S(2)}) collective-permute-start(bf16[1,1,16,3,8192]{4,2,3,1,0:T(8,128)(2,1)S(1)} %collective-permute-done.3), channel_id=1, source_target_pairs={{0,16},{16,32},{32,48},{48,64},{64,80},{80,96},{96,112},{112,128},... | collective-permute-start | bytes 2359304 | tf_op jit(solution)/shard_map/ppermute | solution.py:127
  235.8 5.3 copy-start.11
  235.8 19.5 %collective-permute-start.11 = (bf16[1,1,16,3,8192]{4,2,3,1,0:T(8,128)(2,1)S(1)}, bf16[1,1,16,3,8192]{4,2,3,1,0:T(8,128)(2,1)S(1)}, u32[]{:S(2)}, u32[]{:S(2)}) collective-permute-start(bf16[1,1,16,3,8192]{4,2,3,1,0:T(8,128)(2,1)S(1)} %collective-permute-done.10), channel_id=1, source_target_pairs={{0,240},{16,0},{32,16},{48,32},{64,48},{80,64},{96,80},{112,96},{1... | collective-permute-start | bytes 2359304 | tf_op jit(solution)/shard_map/ppermute | solution.py:129
  255.3 24.3 %copy-start.17 = (bf16[1,1,16,3,8192]{4,2,3,1,0:T(8,128)(2,1)}, bf16[1,1,16,3,8192]{4,2,3,1,0:T(8,128)(2,1)S(1)}, u32[]{:S(2)}) copy-start(bf16[1,1,16,3,8192]{4,2,3,1,0:T(8,128)(2,1)S(1)} %collective-permute-done.4) | copy-start | bytes 2359300
  255.3 18.6 %collective-permute-start.5 = (bf16[1,1,16,3,8192]{4,2,3,1,0:T(8,128)(2,1)S(1)}, bf16[1,1,16,3,8192]{4,2,3,1,0:T(8,128)(2,1)S(1)}, u32[]{:S(2)}, u32[]{:S(2)}) collective-permute-start(bf16[1,1,16,3,8192]{4,2,3,1,0:T(8,128)(2,1)S(1)} %collective-permute-done.4), channel_id=1, source_target_pairs={{0,16},{16,32},{32,48},{48,64},{64,80},{80,96},{96,112},{112,128},... | collective-permute-start | bytes 2359304 | tf_op jit(solution)/shard_map/ppermute | solution.py:127
  255.3 0.9 copy-start.13
  256.2 17.7 %collective-permute-start.12 = (bf16[1,1,16,3,8192]{4,2,3,1,0:T(8,128)(2,1)S(1)}, bf16[1,1,16,3,8192]{4,2,3,1,0:T(8,128)(2,1)}, u32[]{:S(2)}, u32[]{:S(2)}) collective-permute-start(bf16[1,1,16,3,8192]{4,2,3,1,0:T(8,128)(2,1)S(1)} %collective-permute-done.11), channel_id=1, source_target_pairs={{0,240},{16,0},{32,16},{48,32},{64,48},{80,64},{96,80},{112,96},{1... | collective-permute-start | bytes 2359304 | tf_op jit(solution)/shard_map/ppermute | solution.py:129
  273.9 17.8 %copy-start.19 = (bf16[1,1,16,3,8192]{4,2,3,1,0:T(8,128)(2,1)}, bf16[1,1,16,3,8192]{4,2,3,1,0:T(8,128)(2,1)S(1)}, u32[]{:S(2)}) copy-start(bf16[1,1,16,3,8192]{4,2,3,1,0:T(8,128)(2,1)S(1)} %collective-permute-done.5) | copy-start | bytes 2359300
  273.9 17.8 %collective-permute-start.6 = (bf16[1,1,16,3,8192]{4,2,3,1,0:T(8,128)(2,1)S(1)}, bf16[1,1,16,3,8192]{4,2,3,1,0:T(8,128)(2,1)}, u32[]{:S(2)}, u32[]{:S(2)}) collective-permute-start(bf16[1,1,16,3,8192]{4,2,3,1,0:T(8,128)(2,1)S(1)} %collective-permute-done.5), channel_id=1, source_target_pairs={{0,16},{16,32},{32,48},{48,64},{64,80},{80,96},{96,112},{112,128},... | collective-permute-start | bytes 2359304 | tf_op jit(solution)/shard_map/ppermute | solution.py:127
  273.9 17.8 %collective-permute-start.13 = (bf16[1,1,16,3,8192]{4,2,3,1,0:T(8,128)(2,1)}, bf16[1,1,16,3,8192]{4,2,3,1,0:T(8,128)(2,1)}, u32[]{:S(2)}, u32[]{:S(2)}) collective-permute-start(bf16[1,1,16,3,8192]{4,2,3,1,0:T(8,128)(2,1)} %collective-permute-done.12), channel_id=1, source_target_pairs={{0,240},{16,0},{32,16},{48,32},{64,48},{80,64},{96,80},{112,96},{1... | collective-permute-start | bytes 2359304 | tf_op jit(solution)/shard_map/ppermute | solution.py:129
  291.7 17.1 %collective-permute-start.7 = (bf16[1,1,16,3,8192]{4,2,3,1,0:T(8,128)(2,1)}, bf16[1,1,16,3,8192]{4,2,3,1,0:T(8,128)(2,1)}, u32[]{:S(2)}, u32[]{:S(2)}) collective-permute-start(bf16[1,1,16,3,8192]{4,2,3,1,0:T(8,128)(2,1)} %collective-permute-done.6), channel_id=1, source_target_pairs={{0,16},{16,32},{32,48},{48,64},{64,80},{80,96},{96,112},{112,128},... | collective-permute-start | bytes 2359304 | tf_op jit(solution)/shard_map/ppermute | solution.py:127
  291.7 65.4 %copy-start.20 = (bf16[1,1,16,3,8192]{4,2,3,1,0:T(8,128)(2,1)S(1)}, bf16[1,1,16,3,8192]{4,2,3,1,0:T(8,128)(2,1)}, u32[]{:S(2)}) copy-start(bf16[1,1,16,3,8192]{4,2,3,1,0:T(8,128)(2,1)} %copy-done.19) | copy-start | bytes 2359300
  291.7 67.0 %copy-start.18 = (bf16[1,1,16,3,8192]{4,2,3,1,0:T(8,128)(2,1)S(1)}, bf16[1,1,16,3,8192]{4,2,3,1,0:T(8,128)(2,1)}, u32[]{:S(2)}) copy-start(bf16[1,1,16,3,8192]{4,2,3,1,0:T(8,128)(2,1)} %copy-done.17) | copy-start | bytes 2359300
  291.7 68.7 %copy-start.16 = (bf16[1,1,16,3,8192]{4,2,3,1,0:T(8,128)(2,1)S(1)}, bf16[1,1,16,3,8192]{4,2,3,1,0:T(8,128)(2,1)}, u32[]{:S(2)}) copy-start(bf16[1,1,16,3,8192]{4,2,3,1,0:T(8,128)(2,1)} %copy-done.15) | copy-start | bytes 2359300
  291.7 70.4 %copy-start.10 = (bf16[1,1,16,3,8192]{4,2,3,1,0:T(8,128)(2,1)S(1)}, bf16[1,1,16,3,8192]{4,2,3,1,0:T(8,128)(2,1)}, u32[]{:S(2)}) copy-start(bf16[1,1,16,3,8192]{4,2,3,1,0:T(8,128)(2,1)} %copy-done.9) | copy-start | bytes 2359300
  291.7 72.0 %copy-start.6 = (bf16[1,1,16,3,8192]{4,2,3,1,0:T(8,128)(2,1)S(1)}, bf16[1,1,16,3,8192]{4,2,3,1,0:T(8,128)(2,1)}, u32[]{:S(2)}) copy-start(bf16[1,1,16,3,8192]{4,2,3,1,0:T(8,128)(2,1)} %copy-done.5) | copy-start | bytes 2359300
  291.7 73.7 %copy-start.2 = (bf16[1,1,16,3,8192]{4,2,3,1,0:T(8,128)(2,1)S(1)}, bf16[1,1,16,3,8192]{4,2,3,1,0:T(8,128)(2,1)}, u32[]{:S(2)}) copy-start(bf16[1,1,16,3,8192]{4,2,3,1,0:T(8,128)(2,1)} %copy-done.1) | copy-start | bytes 2359300
  291.7 76.9 %copy-start.4 = (bf16[1,1,16,3,8192]{4,2,3,1,0:T(8,128)(2,1)S(1)}, bf16[1,1,16,3,8192]{4,2,3,1,0:T(8,128)(2,1)}, u32[]{:S(2)}) copy-start(bf16[1,1,16,3,8192]{4,2,3,1,0:T(8,128)(2,1)} %copy-done.3) | copy-start | bytes 2359300
  291.7 78.5 %copy-start.8 = (bf16[1,1,16,3,8192]{4,2,3,1,0:T(8,128)(2,1)S(1)}, bf16[1,1,16,3,8192]{4,2,3,1,0:T(8,128)(2,1)}, u32[]{:S(2)}) copy-start(bf16[1,1,16,3,8192]{4,2,3,1,0:T(8,128)(2,1)} %copy-done.7) | copy-start | bytes 2359300
  291.7 80.2 %copy-start.12 = (bf16[1,1,16,3,8192]{4,2,3,1,0:T(8,128)(2,1)S(1)}, bf16[1,1,16,3,8192]{4,2,3,1,0:T(8,128)(2,1)}, u32[]{:S(2)}) copy-start(bf16[1,1,16,3,8192]{4,2,3,1,0:T(8,128)(2,1)} %copy-done.11) | copy-start | bytes 2359300
  291.8 81.9 %copy-start.14 = (bf16[1,1,16,3,8192]{4,2,3,1,0:T(8,128)(2,1)S(1)}, bf16[1,1,16,3,8192]{4,2,3,1,0:T(8,128)(2,1)}, u32[]{:S(2)}) copy-start(bf16[1,1,16,3,8192]{4,2,3,1,0:T(8,128)(2,1)} %copy-done.13) | copy-start | bytes 2359300
  291.8 57.7 %collective-permute-start.14 = (bf16[1,1,16,3,8192]{4,2,3,1,0:T(8,128)(2,1)}, bf16[1,1,16,3,8192]{4,2,3,1,0:T(8,128)(2,1)S(1)}, u32[]{:S(2)}, u32[]{:S(2)}) collective-permute-start(bf16[1,1,16,3,8192]{4,2,3,1,0:T(8,128)(2,1)} %collective-permute-done.13), channel_id=1, source_target_pairs={{0,240},{16,0},{32,16},{48,32},{64,48},{80,64},{96,80},{112,96},{1... | collective-permute-start | bytes 2359304 | tf_op jit(solution)/shard_map/ppermute | solution.py:129
  420.9 129.0 %copy-start.21 = (s32[16,2]{0,1:T(2,128)S(1)}, s32[16,2]{0,1:T(2,128)}, u32[]{:S(2)}) copy-start(s32[16,2]{0,1:T(2,128)} %param.29) | copy-start | bytes 388
  420.9 129.2 %copy-start.22 = (f32[16,2]{0,1:T(2,128)S(1)}, f32[16,2]{0,1:T(2,128)}, u32[]{:S(2)}) copy-start(f32[16,2]{0,1:T(2,128)} %param.30) | copy-start | bytes 388
  542.0 35.9 %all-to-all-start.2 = ((bf16[1,1,16,3,8192]{4,3,1,0,2:T(4,128)(2,1)}), bf16[1,1,16,3,8192]{4,3,1,0,2:T(4,128)(2,1)}, u32[]{:S(2)}, u32[]{:S(2)}) async-start(bf16[1,1,16,3,8192]{4,3,1,0,2:T(4,128)(2,1)} %copy.122), calls=%async_computation.2 | async-start | bytes 2097152 | tf_op jit(solution)/shard_map/all_to_all | solution.py:139
Sparse Core Ops, SparseCore 0:
  14.1 52.8 all-gather.3
  443.1 96.0 reduce-scatter.6
